TPU v7x, 512 devices: a whole 4x4x16 slice. The times are simulated.
512 devices in a mesh: expert: 32 (over z, x_lo), fsdp: 16 (over x_hi, y, core).
Axes of the slice: x: 4 (x_hi: 2, x_lo: 2; x = x_hi * 2 + x_lo), y: 4, z: 16, core: 2. Of those that a mesh axis runs over, the one named last changes fastest.
Arguments:
- tokens: bfloat16 [3584, 4096], P(('expert', 'fsdp')), may hold values from -6 to 6
- expert_ids: int32 [3584, 8], P(('expert', 'fsdp')), may hold values from 0 to 31, all different within a row; in each aligned block of 7 rows (0 to 6, 7 to 13, ...) at most 2 rows name the same one
- gate_scores: float32 [3584, 8], P(('expert', 'fsdp')), may hold values from 0.05 to 1
- w_gate: bfloat16 [32, 1536, 4096], P('expert', 'fsdp'), may hold values from -0.09375 to 0.09375
- w_up: bfloat16 [32, 1536, 4096], P('expert', 'fsdp'), may hold values from -0.09375 to 0.09375
- w_down: bfloat16 [32, 1536, 4096], P('expert', None, 'fsdp'), may hold values from -0.15625 to 0.15625
Outputs:
- mixed: bfloat16 [3584, 4096], P(('expert', 'fsdp'))
Inputs may be any that keep to these rules, and one draw needn't show every extreme that they name: `expert_ids`: each token names 8 different experts. Within the 7 tokens of one device (aligned blocks of rows) no expert is named more than 2 times, and in every draw some expert is named exactly 2 times in some block.
All inputs are finite; a program needn't handle non-finite values.
Results may differ from a plain program's by a relative error of at most 0.0057.
Values may be sent and summed in bfloat16 or wider, within the bound.
A program may use at most 64 MiB of HBM per device.

v0:
```python
import jax
import jax.numpy as jnp
from jax import lax
from jax.sharding import PartitionSpec as P


def on_device(tokens, expert_ids, gate_scores, w_gate, w_up, w_down):
    n_expert = lax.axis_size("expert")
    n_fsdp = lax.axis_size("fsdp")
    local_tok, top_k = expert_ids.shape
    per_column = w_gate.shape[0]
    experts = per_column * n_expert
    capacity = min(local_tok, max(2, 3 * local_tok * top_k // (2 * experts)))
    width = tokens.shape[1]
    feature_cols = w_down.shape[2]
    weights = gate_scores / jnp.sum(gate_scores, axis=1, keepdims=True)
    expert_iota = lax.broadcasted_iota(jnp.int32, (1, 1, experts), 2)
    matches = (expert_ids[:, :, None] == expert_iota).astype(jnp.int32)
    chosen = jnp.sum(matches, axis=1, dtype=jnp.int32)
    weight_table = jnp.sum(weights[:, :, None] * matches.astype(jnp.float32), axis=1)
    ranks = jnp.cumsum(chosen, axis=0, dtype=jnp.int32) - chosen
    slot_iota = lax.broadcasted_iota(jnp.int32, (1, 1, capacity), 2)
    slot_mask = jnp.logical_and(ranks[:, :, None] == slot_iota, chosen[:, :, None] > 0)
    select_f32 = jnp.transpose(slot_mask.astype(jnp.float32), (1, 2, 0))
    select_bf = select_f32.astype(jnp.bfloat16)
    combine_table = select_f32 * jnp.transpose(weight_table)[:, None, :]
    outgoing = jnp.einsum("ect,td->ecd", select_bf, tokens, preferred_element_type=jnp.float32)
    outgoing = outgoing.astype(jnp.bfloat16)
    arrived = lax.all_to_all(outgoing, "expert", split_axis=0, concat_axis=0, tiled=True)
    portion = lax.all_gather(arrived[None], "fsdp", axis=0, tiled=True)
    routed = portion.reshape(portion.shape[0], n_expert, per_column, capacity, width)
    gate_act = jnp.einsum("knjcd,jhd->knjch", routed, w_gate, preferred_element_type=jnp.float32)
    up_act = jnp.einsum("knjcd,jhd->knjch", routed, w_up, preferred_element_type=jnp.float32)
    hidden = (jax.nn.silu(gate_act) * up_act).astype(jnp.bfloat16)
    summed = jnp.einsum(
        "fnjch,jhd->fnjcd",
        lax.all_gather(hidden, "fsdp", axis=4, tiled=True),
        w_down,
        preferred_element_type=jnp.float32,
    )
    expert_out = summed.astype(jnp.bfloat16).reshape(
        n_fsdp, n_expert, per_column * capacity, feature_cols
    )
    returned = lax.all_to_all(
        lax.all_to_all(expert_out, "expert", split_axis=1, concat_axis=1, tiled=True),
        "fsdp",
        split_axis=0,
        concat_axis=3,
        tiled=True,
    )
    returned = returned.reshape(experts, capacity, width)
    mixed = jnp.einsum(
        "ect,ecd->td", combine_table, returned.astype(jnp.float32), precision=lax.Precision.HIGHEST
    )
    return mixed.astype(jnp.bfloat16)


def solution(mesh):
    placed = (
        P(("expert", "fsdp"), None),
        P(("expert", "fsdp"), None),
        P(("expert", "fsdp"), None),
        P("expert", "fsdp", None),
        P("expert", "fsdp", None),
        P("expert", None, "fsdp"),
    )
    return jax.shard_map(
        on_device,
        mesh=mesh,
        in_specs=placed,
        out_specs=P(("expert", "fsdp"), None),
        check_vma=False,
    )
```

profile of v0, /device:TPU:1, one launch (start us, length us, event | category | flops | bytes accessed | tf_op | source)
XLA Modules:
  0.0 343.0 jit_solution(12220957122521888835)
XLA Ops:
  6.5 0.8 convert_reduce_fusion
  7.4 1.2 convolution_convert_fusion
  8.6 0.5 copy.34
  9.2 48.1 %all_to_all.25 = bf16[32,2,4096]{2,1,0:T(2,128)(2,1)S(1)} all-to-all(bf16[32,2,4096]{2,1,0:T(2,128)(2,1)S(1)} %copy.34), channel_id=1, replica_groups=mesh['expert'=32,'fsdp'=16] {'expert'}, dimensions={0} | all-to-all | bytes 1048576 | tf_op jit(solution)/shard_map/all_to_all | solution.py:29
  57.3 1.1 copy.35
  58.5 82.3 %all-gather.6.cloned.1.call-done = bf16[512,2,4096]{2,0,1:T(8,128)(2,1)} async-done(((bf16[32,2,4096]{2,0,1:T(8,128)(2,1)}), bf16[512,2,4096]{2,0,1:T(8,128)(2,1)}) %all-gather.6.cloned.1.call-update) | async-done | bytes 8388624 | tf_op jit(solution)/shard_map/all_gather | solution.py:30
  140.8 6.0 %fusion.10 = f32[16,32,1,2,96]{4,1,3,0,2:T(8,128)S(1)} fusion(bf16[16,32,2,4096]{3,1,0,2:T(8,128)(2,1)} %bitcast.65, bf16[1,96,4096]{2,1,0:T(8,128)(2,1)} %param.9), kind=kOutput, calls=%fused_computation.10 | convolution fusion | flops 805306368 | bytes 9568256 | tf_op jit(solution)/shard_map/knjcd,jhd->knjch/dot_general | solution.py:32
  146.8 0.1 copy-done.4
  146.9 2.3 fusion.19
  149.3 2.1 copy.38
  151.4 103.8 %all-gather.4.cloned.1.call-done = bf16[16,32,1,2,1536]{1,0,3,2,4:T(8,128)(2,1)} async-done(((bf16[16,32,1,2,96]{1,0,3,2,4:T(8,128)(2,1)}), bf16[16,32,1,2,1536]{1,0,3,2,4:T(8,128)(2,1)}) %all-gather.4.cloned.1.call-update) | async-done | bytes 3145744 | tf_op jit(solution)/shard_map/all_gather | solution.py:37
  255.2 13.4 %copy.39 = bf16[16,32,1,2,1536]{4,1,3,0,2:T(8,128)(2,1)} copy(bf16[16,32,1,2,1536]{1,0,3,2,4:T(8,128)(2,1)} %all-gather.4.cloned.1.call-done) | data formatting | bytes 6291456 | tf_op jit(solution)/shard_map/all_gather | solution.py:37
  268.6 2.9 fusion.7
  271.5 0.5 copy.40
  272.0 44.3 %all_to_all.26 = bf16[16,32,2,256]{3,2,0,1:T(2,128)(2,1)S(1)} all-to-all(bf16[16,32,2,256]{3,2,0,1:T(2,128)(2,1)S(1)} %copy.40), channel_id=1, replica_groups=mesh['expert'=32,'fsdp'=16] {'expert'}, dimensions={1} | all-to-all | bytes 1048576 | tf_op jit(solution)/shard_map/all_to_all | solution.py:45
  316.4 1.3 copy.41
  317.7 5.8 %all-to-all-start.2 = ((bf16[16,32,2,256]{3,2,1,0:T(2,128)(2,1)}), bf16[16,32,2,256]{3,2,1,0:T(2,128)(2,1)S(1)}, u32[]{:S(2)}, u32[]{:S(2)}) async-start(bf16[16,32,2,256]{3,2,1,0:T(2,128)(2,1)} %copy.41), calls=%async_computation.2 | async-start | bytes 1048576 | tf_op jit(solution)/shard_map/all_to_all | solution.py:44
  323.4 0.1 reduce_sum.28
  323.6 0.1 broadcast_divide_fusion
  323.6 0.1 fusion.27
  323.7 10.9 %all-to-all-done.2 = bf16[16,32,2,256]{3,2,1,0:T(2,128)(2,1)S(1)} async-done(((bf16[16,32,2,256]{3,2,1,0:T(2,128)(2,1)}), bf16[16,32,2,256]{3,2,1,0:T(2,128)(2,1)S(1)}, u32[]{:S(2)}, u32[]{:S(2)}) %all-to-all-start.2) | async-done | bytes 524320 | tf_op jit(solution)/shard_map/all_to_all | solution.py:44
  334.6 0.3 copy.42
  334.9 0.2 reshape.47
  335.2 1.0 fusion.4
  (16 shorter events, 0.1 us)
Async XLA Ops:
  6.5 262.1 %copy-start = (bf16[1,1536,256]{2,1,0:T(8,128)(2,1)S(1)}, bf16[1,1536,256]{2,1,0:T(8,128)(2,1)}, u32[]{:S(2)}) copy-start(bf16[1,1536,256]{2,1,0:T(8,128)(2,1)} %param.11) | copy-start | bytes 2359300
  6.5 134.3 %all-gather.6.cloned.1.call-start = ((), (), s32[]{:S(2)}) async-start(), calls=%async_computation.4 | async-start | bytes 8912896 | tf_op jit(solution)/shard_map/all_gather | solution.py:30
  58.4 196.7 %all-gather.4.cloned.1.call-start = ((), (), s32[]{:S(2)}) async-start(), calls=%async_computation.3 | async-start | bytes 13369344 | tf_op jit(solution)/shard_map/all_gather | solution.py:37
  140.8 6.0 %copy-start.3 = (bf16[512,2,4096]{2,0,1:T(8,128)(2,1)S(1)}, bf16[512,2,4096]{2,0,1:T(8,128)(2,1)}, u32[]{:S(2)}) copy-start(bf16[512,2,4096]{2,0,1:T(8,128)(2,1)} %all-gather.6.cloned.1.call-done) | copy-start | bytes 25165828
  140.8 6.1 %copy-start.4 = (bf16[1,96,4096]{2,1,0:T(8,128)(2,1)S(1)}, bf16[1,96,4096]{2,1,0:T(8,128)(2,1)}, u32[]{:S(2)}) copy-start(bf16[1,96,4096]{2,1,0:T(8,128)(2,1)} %param.10) | copy-start | bytes 2359300
  268.6 54.9 %copy-start.2 = (f32[7,8]{1,0:T(8,128)S(1)}, f32[7,8]{1,0:T(8,128)}, u32[]{:S(2)}) copy-start(f32[7,8]{1,0:T(8,128)} %param.8) | copy-start | bytes 676
  268.6 55.1 %copy-start.1 = (s32[7,8]{1,0:T(8,128)S(1)}, s32[7,8]{1,0:T(8,128)}, u32[]{:S(2)}) copy-start(s32[7,8]{1,0:T(8,128)} %param.7) | copy-start | bytes 676
  317.7 16.9 %all-to-all-start.2 = ((bf16[16,32,2,256]{3,2,1,0:T(2,128)(2,1)}), bf16[16,32,2,256]{3,2,1,0:T(2,128)(2,1)S(1)}, u32[]{:S(2)}, u32[]{:S(2)}) async-start(bf16[16,32,2,256]{3,2,1,0:T(2,128)(2,1)} %copy.41), calls=%async_computation.2 | async-start | bytes 1048576 | tf_op jit(solution)/shard_map/all_to_all | solution.py:44
Sparse Core Ops, SparseCore 0:
  58.6 82.1 all-gather.5
  151.5 103.6 all-gather.3
where the time goes:
time: 344 us; the launch traced here: 343 us
  waiting for transfers between devices  197 us (57%)
  blocking collectives  92.5 us (27%)
  local copies, waits for them, and re-layouts  19.6 us (6%)
  between operations  13.5 us (4%)
  matrix products  13.4 us (4%)
  starting transfers between devices  5.81 us (2%)
    all_gather x1, waiting for transfers between devices, on_device(): lax.all_gather(hidden, 'fsdp', axis=4, tiled=True)  104 us
    all_gather x1, waiting for transfers between devices, on_device(): portion = lax.all_gather(arrived[None], 'fsdp', axis=0, tiled=True)  82.3 us
    all_to_all x1, blocking collectives, on_device(): lax.all_to_all(outgoing, 'expert', split_axis=0, concat_axis=0, tiled=True)  48.1 us
    all_to_all x1, blocking collectives, on_device(): lax.all_to_all(expert_out, 'expert', split_axis=1, concat_axis=1, tiled=T...  44.3 us
    all_gather x1, local copies, waits for them, and re-layouts, on_device(): lax.all_gather(hidden, 'fsdp', axis=4, tiled=True)  13.4 us
    all_to_all x1, waiting for transfers between devices, on_device(): lax.all_to_all(lax.all_to_all(expert_out, 'expert', split_axis=1, concat_...  10.9 us
  transfers between devices with their start and end apart: 3, of which 3 were waited for; matrix products, arithmetic and copies ran while one was open for 0% of the time, Pallas kernels for 0%

commit v1 on v0

--- a/solution.py
+++ b/solution.py
@@ -34,7 +34,9 @@
     hidden = (jax.nn.silu(gate_act) * up_act).astype(jnp.bfloat16)
     summed = jnp.einsum(
         "fnjch,jhd->fnjcd",
-        lax.all_gather(hidden, "fsdp", axis=4, tiled=True),
+        jnp.concatenate(
+            lax.all_to_all(jnp.stack([hidden] * lax.axis_size("fsdp")), "fsdp", 0, 0), axis=4
+        ),
         w_down,
         preferred_element_type=jnp.float32,
     )

time: 344 us -> 296 us (0.86)
  waiting for transfers between devices: 197 us -> 93.3 us
  blocking collectives: 92.5 us -> 145 us
    all_gather x1 -> x0, waiting for transfers between devices: 104 us -> none  [on_device(): lax.all_gather(hidden, 'fsdp', axis=4, tiled=True)]
    all_to_all x0 -> x1, blocking collectives: none -> 53.3 us  [on_device(): lax.all_to_all(jnp.stack([hidden] * lax.axis_size('fsdp')), 'fsdp', 0, 0)]
    all_gather x1 -> x0, local copies, waits for them, and re-layouts: 13.4 us -> none  [on_device(): lax.all_gather(hidden, 'fsdp', axis=4, tiled=True)]
    another operation x0 -> x2, local copies, waits for them, and re-layouts: none -> 9.13 us
    reshape x0 -> x1, local copies, waits for them, and re-layouts: none -> 8.6 us  [on_device(): jnp.concatenate(lax.all_to_all(jnp.stack([hidden] * lax.axis_size('fsdp')...]
  transfers between devices with their start and end apart: 3 -> 2, of which waited for: 3 -> 2; matrix products, arithmetic and copies ran while one was open for 0% -> 0% of each run, Pallas kernels for 0% -> 0%
where the time goes in v1:
time: 296 us
  blocking collectives  145 us (49%)
  waiting for transfers between devices  93.3 us (32%)
  local copies, waits for them, and re-layouts  21.9 us (7%)
  matrix products  13.5 us (5%)
  between operations  13.5 us (5%)
  starting transfers between devices  7.53 us (3%)
    all_gather x1, waiting for transfers between devices, on_device(): portion = lax.all_gather(arrived[None], 'fsdp', axis=0, tiled=True)  82.4 us
    all_to_all x1, blocking collectives, on_device(): lax.all_to_all(jnp.stack([hidden] * lax.axis_size('fsdp')), 'fsdp', 0, 0)  53.3 us
    all_to_all x1, blocking collectives, on_device(): lax.all_to_all(outgoing, 'expert', split_axis=0, concat_axis=0, tiled=True)  48.1 us
    all_to_all x1, blocking collectives, on_device(): lax.all_to_all(expert_out, 'expert', split_axis=1, concat_axis=1, tiled=T...  43.5 us
    all_to_all x1, waiting for transfers between devices, on_device(): lax.all_to_all(lax.all_to_all(expert_out, 'expert', split_axis=1, concat_...  10.9 us
    reshape x1, local copies, waits for them, and re-layouts, on_device(): jnp.concatenate(lax.all_to_all(jnp.stack([hidden] * lax.axis_size('fsdp')...  8.6 us
    another operation x1, local copies, waits for them, and re-layouts  8.08 us
    all_to_all x1, starting transfers between devices, on_device(): lax.all_to_all(lax.all_to_all(expert_out, 'expert', split_axis=1, concat_...  7.52 us
  transfers between devices with their start and end apart: 2, of which 2 were waited for; matrix products, arithmetic and copies ran while one was open for 0% of the time, Pallas kernels for 0%

profile of v1, /device:TPU:1, one launch (start us, length us, event | category | flops | bytes accessed | tf_op | source)
XLA Modules:
  0.0 295.6 jit_solution(973012164334601140)
XLA Ops:
  6.5 0.8 convert_reduce_fusion
  7.4 1.2 convolution_convert_fusion
  8.6 0.5 copy.31
  9.2 48.1 %all_to_all.30 = bf16[32,2,4096]{2,1,0:T(2,128)(2,1)S(1)} all-to-all(bf16[32,2,4096]{2,1,0:T(2,128)(2,1)S(1)} %copy.31), channel_id=1, replica_groups=mesh['expert'=32,'fsdp'=16] {'expert'}, dimensions={0} | all-to-all | bytes 1048576 | tf_op jit(solution)/shard_map/all_to_all | solution.py:29
  57.3 1.1 copy.32
  58.4 82.4 %all-gather.3.cloned.1.call-done = bf16[512,2,4096]{2,0,1:T(8,128)(2,1)} async-done(((bf16[32,2,4096]{2,0,1:T(8,128)(2,1)}), bf16[512,2,4096]{2,0,1:T(8,128)(2,1)}) %all-gather.3.cloned.1.call-update) | async-done | bytes 8388624 | tf_op jit(solution)/shard_map/all_gather | solution.py:30
  140.8 6.0 %fusion.5 = f32[16,32,1,2,96]{4,1,3,0,2:T(8,128)S(1)} fusion(bf16[16,32,2,4096]{3,1,0,2:T(8,128)(2,1)} %bitcast.71, bf16[1,96,4096]{2,1,0:T(8,128)(2,1)} %param.9), kind=kOutput, calls=%fused_computation.8 | convolution fusion | flops 805306368 | bytes 9568256 | tf_op jit(solution)/shard_map/knjcd,jhd->knjch/dot_general | solution.py:32
  146.8 0.1 copy-done.4
  146.9 2.4 fusion.17
  149.3 1.1 stack.2
  150.4 53.3 %all_to_all.31 = bf16[16,16,32,1,2,96]{5,2,4,1,3,0:T(8,128)(2,1)S(1)} all-to-all(bf16[16,16,32,1,2,96]{5,2,4,1,3,0:T(8,128)(2,1)S(1)} %stack.2), channel_id=1, replica_groups=mesh['expert'=32,'fsdp'=16] {'fsdp'}, dimensions={0} | all-to-all | bytes 6291456 | tf_op jit(solution)/shard_map/all_to_all | solution.py:38
  203.7 8.6 %copy.35 = bf16[16,32,1,2,16,96]{5,4,1,3,0,2:T(8,128)(2,1)} copy(bf16[16,32,1,2,16,96]{5,1,3,0,2,4:T(8,128)(2,1)S(1)} %bitcast.68) | data formatting | bytes 6291456 | tf_op jit(solution)/shard_map/reshape | solution.py:37
  212.3 8.1 %reshape.54 = bf16[16,32,2,1536]{3,1,2,0:T(8,128)(2,1)} reshape(bf16[16,32,1,2,16,96]{5,4,1,3,0,2:T(8,128)(2,1)} %copy.35) | data formatting | bytes 6291456 | tf_op jit(solution)/shard_map/reshape.13
  220.4 2.9 convolution_convert_fusion.1
  223.2 0.5 copy.36
  223.8 43.5 %all_to_all.32 = bf16[16,32,2,256]{3,2,0,1:T(2,128)(2,1)S(1)} all-to-all(bf16[16,32,2,256]{3,2,0,1:T(2,128)(2,1)S(1)} %copy.36), channel_id=1, replica_groups=mesh['expert'=32,'fsdp'=16] {'expert'}, dimensions={1} | all-to-all | bytes 1048576 | tf_op jit(solution)/shard_map/all_to_all | solution.py:47
  267.2 1.3 copy.37
  268.5 7.5 %all-to-all-start.3 = ((bf16[16,32,2,256]{3,2,1,0:T(2,128)(2,1)}), bf16[16,32,2,256]{3,2,1,0:T(2,128)(2,1)S(1)}, u32[]{:S(2)}, u32[]{:S(2)}) async-start(bf16[16,32,2,256]{3,2,1,0:T(2,128)(2,1)} %copy.37), calls=%async_computation.3 | async-start | bytes 1048576 | tf_op jit(solution)/shard_map/all_to_all | solution.py:46
  276.1 0.1 reduce_sum.28
  276.3 0.1 fusion.25
  276.4 10.9 %all-to-all-done.3 = bf16[16,32,2,256]{3,2,1,0:T(2,128)(2,1)S(1)} async-done(((bf16[16,32,2,256]{3,2,1,0:T(2,128)(2,1)}), bf16[16,32,2,256]{3,2,1,0:T(2,128)(2,1)S(1)}, u32[]{:S(2)}, u32[]{:S(2)}) %all-to-all-start.3) | async-done | bytes 524320 | tf_op jit(solution)/shard_map/all_to_all | solution.py:46
  287.2 0.3 copy.38
  287.5 0.2 reshape.56
  287.8 1.0 fusion.4
  (15 shorter events, 0.1 us)
Async XLA Ops:
  6.5 213.8 %copy-start = (bf16[1,1536,256]{2,1,0:T(8,128)(2,1)S(1)}, bf16[1,1536,256]{2,1,0:T(8,128)(2,1)}, u32[]{:S(2)}) copy-start(bf16[1,1536,256]{2,1,0:T(8,128)(2,1)} %param.11) | copy-start | bytes 2359300
  6.5 134.3 %all-gather.3.cloned.1.call-start = ((), (), s32[]{:S(2)}) async-start(), calls=%async_computation.4 | async-start | bytes 8912896 | tf_op jit(solution)/shard_map/all_gather | solution.py:30
  140.8 6.0 %copy-start.3 = (bf16[512,2,4096]{2,0,1:T(8,128)(2,1)S(1)}, bf16[512,2,4096]{2,0,1:T(8,128)(2,1)}, u32[]{:S(2)}) copy-start(bf16[512,2,4096]{2,0,1:T(8,128)(2,1)} %all-gather.3.cloned.1.call-done) | copy-start | bytes 25165828
  140.8 6.1 %copy-start.4 = (bf16[1,96,4096]{2,1,0:T(8,128)(2,1)S(1)}, bf16[1,96,4096]{2,1,0:T(8,128)(2,1)}, u32[]{:S(2)}) copy-start(bf16[1,96,4096]{2,1,0:T(8,128)(2,1)} %param.10) | copy-start | bytes 2359300
  212.3 63.8 %copy-start.2 = (f32[7,8]{1,0:T(8,128)S(1)}, f32[7,8]{1,0:T(8,128)}, u32[]{:S(2)}) copy-start(f32[7,8]{1,0:T(8,128)} %param.8) | copy-start | bytes 676
  212.3 64.0 %copy-start.1 = (s32[7,8]{1,0:T(8,128)S(1)}, s32[7,8]{1,0:T(8,128)}, u32[]{:S(2)}) copy-start(s32[7,8]{1,0:T(8,128)} %param.7) | copy-start | bytes 676
  268.5 18.7 %all-to-all-start.3 = ((bf16[16,32,2,256]{3,2,1,0:T(2,128)(2,1)}), bf16[16,32,2,256]{3,2,1,0:T(2,128)(2,1)S(1)}, u32[]{:S(2)}, u32[]{:S(2)}) async-start(bf16[16,32,2,256]{3,2,1,0:T(2,128)(2,1)} %copy.37), calls=%async_computation.3 | async-start | bytes 1048576 | tf_op jit(solution)/shard_map/all_to_all | solution.py:46
Sparse Core Ops, SparseCore 0:
  58.5 82.2 all-gather.2
